TPU v7x, 32 devices: a whole 2x2x4 slice. The times are simulated.
32 devices in a mesh: shard: 8 (over z, y), tensor: 4 (over x, core).
Axes of the slice: x: 2, y: 2, z: 4, core: 2. Of those that a mesh axis runs over, the one named last changes fastest.
Arguments:
- acts: bfloat16 [2048, 1152], P('shard', 'tensor'), may hold values from -600 to 600
- outgrads: bfloat16 [2048, 1152], P('shard', 'tensor'), may hold values from -800 to 800
- weight: bfloat16 [1152, 1152], P('shard', 'tensor'), may hold values from -6 to 6
- momentum: float32 [1152, 1152], P('shard', 'tensor'), may hold values from -6 to 6
- damping: float32 [2], replicated, may hold values from 0.3 to 3
- coeffs: float32 [4], replicated, may hold values from 0.5 to 2
Outputs:
- new_momentum: float32 [1152, 1152], P('shard', 'tensor')
- gathered_weight: bfloat16 [1152, 1152], P(None, 'tensor')
All inputs are finite; a program needn't handle non-finite values.
Results may differ from a plain program's by a relative error of at most 0.003.
The roundings to bfloat16 on the way count: a program that leaves them out, or rounds other values in their place, can miss the bound.
Values may be sent and summed in bfloat16 or wider, within the bound.
A program may use at most 64 MiB of HBM per device.

v0:
```python
import jax
import jax.numpy as jnp
from jax import lax
from jax.sharding import PartitionSpec as P

D = 1152


def horner_columns(factor, coeffs, first_col, col_count, bound_norm):
    extent = factor.shape[0]
    row_ids = lax.broadcasted_iota(jnp.int32, (extent, col_count), 0)
    col_ids = lax.broadcasted_iota(jnp.int32, (extent, col_count), 1) + first_col
    identity_cols = (row_ids == col_ids).astype(jnp.float32)
    term_count = coeffs.shape[0]
    iterate = coeffs[term_count - 1] * identity_cols
    for term_index in range(term_count - 2, -1, -1):
        product = jnp.dot(factor, iterate.astype(jnp.bfloat16), preferred_element_type=jnp.float32)
        iterate = coeffs[term_index] * identity_cols + iterate - product / bound_norm
    return iterate


def tokens_product(left, right):
    return lax.dot_general(
        left, right, (((0,), (0,)), ((), ())), preferred_element_type=jnp.float32
    )


def on_device(acts, outgrads, weight, momentum, damping, coeffs):
    row_count = weight.shape[0]
    col_count = weight.shape[1]
    row_first = lax.axis_index("shard") * row_count
    col_first = lax.axis_index("tensor") * col_count
    full_acts, full_grads = (
        lax.all_gather(acts, "tensor", axis=1, tiled=True),
        lax.all_gather(outgrads, "tensor", axis=1, tiled=True),
    )
    local_squares = jnp.stack(
        [
            jnp.sum(jnp.square(acts.astype(jnp.float32))),
            jnp.sum(jnp.square(outgrads.astype(jnp.float32))),
        ]
    )
    traces = lax.psum(local_squares, ("shard", "tensor"))
    act_part = tokens_product(full_acts, acts)
    grad_part = tokens_product(full_grads, outgrads)
    stats = lax.psum_scatter(
        jnp.concatenate([act_part, grad_part], axis=1), "shard", scatter_dimension=0, tiled=True
    )
    row_ids = lax.broadcasted_iota(jnp.int32, (row_count, col_count), 0) + row_first
    col_ids = lax.broadcasted_iota(jnp.int32, (row_count, col_count), 1) + col_first
    diag_mask = (row_ids == col_ids).astype(jnp.float32)
    act_piece = (stats[:, :col_count] + damping[0] * traces[0] / D * diag_mask).astype(jnp.bfloat16)
    grad_piece = (stats[:, col_count:] + damping[1] * traces[1] / D * diag_mask).astype(
        jnp.bfloat16
    )
    act_wide, grad_wide = (
        lax.all_gather(act_piece, "tensor", axis=1, tiled=True),
        lax.all_gather(grad_piece, "tensor", axis=1, tiled=True),
    )
    act_full, grad_full = (
        lax.all_gather(act_wide, "shard", axis=0, tiled=True),
        lax.all_gather(grad_wide, "shard", axis=0, tiled=True),
    )
    act_scale = jnp.sqrt(jnp.sum(jnp.square(act_full.astype(jnp.float32))))
    grad_scale = jnp.sqrt(jnp.sum(jnp.square(grad_full.astype(jnp.float32))))
    act_inverse = horner_columns(act_full, coeffs, row_first, row_count, act_scale)
    grad_inverse = horner_columns(grad_full, coeffs, col_first, col_count, grad_scale).astype(
        jnp.bfloat16
    )
    projected = jnp.dot(full_grads, grad_inverse, preferred_element_type=jnp.float32).astype(
        jnp.bfloat16
    )
    right_term = tokens_product(full_acts, projected)
    right_product = lax.psum(right_term, "shard")
    update = lax.dot_general(
        act_inverse,
        right_product,
        (((0,), (0,)), ((), ())),
        precision=lax.Precision.HIGHEST,
        preferred_element_type=jnp.float32,
    )
    square_sum = lax.psum(jnp.sum(update * update), ("shard", "tensor"))
    mean_square = square_sum / (D * D)
    new_momentum = 0.9 * momentum + update / jnp.sqrt(mean_square + 1e-06)
    new_weight = (weight.astype(jnp.float32) - 0.1 * new_momentum).astype(jnp.bfloat16)
    gathered_weight = lax.all_gather(new_weight, "shard", axis=0, tiled=True)
    return (new_momentum, gathered_weight)


def solution(mesh):
    in_specs = (
        P("shard", "tensor"),
        P("shard", "tensor"),
        P("shard", "tensor"),
        P("shard", "tensor"),
        P(),
        P(),
    )
    out_specs = (P("shard", "tensor"), P(None, "tensor"))
    return jax.shard_map(
        on_device, mesh=mesh, in_specs=in_specs, out_specs=out_specs, check_vma=False
    )
```

profile of v0, /device:TPU:0, one launch (start us, length us, event | category | flops | bytes accessed | tf_op | source)
XLA Modules:
  0.0 394.1 jit_solution(14097497905494058269)
XLA Ops:
  7.2 9.2 %all_gather.21 = bf16[256,1152]{0,1:T(8,128)(2,1)S(1)} all-gather(bf16[256,288]{0,1:T(8,128)(2,1)} %param.6), channel_id=1, replica_groups=mesh['shard'=8,'tensor'=4] {'tensor'}, dimensions={1}, use_global_device_ids=true | all-gather | bytes 737280 | tf_op jit(solution)/shard_map/all_gather | solution.py:34
  16.4 1.3 fusion.37
  17.7 7.6 %all_gather.22 = bf16[256,1152]{0,1:T(8,128)(2,1)S(1)} all-gather(bf16[256,288]{0,1:T(8,128)(2,1)S(1)} %copy-done.4), channel_id=1, replica_groups=mesh['shard'=8,'tensor'=4] {'tensor'}, dimensions={1}, use_global_device_ids=true | all-gather | bytes 737280 | tf_op jit(solution)/shard_map/all_gather | solution.py:35
  26.7 2.3 copy.17
  31.4 1.4 pad_maximum_fusion.1
  32.7 41.5 %psum.21 = f32[2]{0:T(128)S(1)} all-reduce(f32[2]{0:T(128)S(1)} %pad_maximum_fusion.1), channel_id=1, replica_groups=mesh['shard'=8,'tensor'=4] {'shard','tensor'}, use_global_device_ids=true, to_apply=%region_3.0 | all-reduce | flops 2 | bytes 16 | tf_op jit(solution)/shard_map/psum | solution.py:43
  78.0 25.5 %reduce-scatter.4.cloned.1.call-done = f32[144,576]{1,0:T(8,128)} async-done(((f32[1152,576]{1,0:T(8,128)}), f32[144,576]{1,0:T(8,128)}) %reduce-scatter.4.cloned.1.call-update) | async-done | bytes 331792
  105.2 6.7 %all-gather.1 = bf16[4,288,144]{1,2,0:T(8,128)(2,1)S(1)} all-gather(bf16[1,288,144]{1,2,0:T(8,128)(2,1)S(1)} %copy.14), channel_id=1, replica_groups=mesh['shard'=8,'tensor'=4] {'tensor'}, dimensions={0}, use_global_device_ids=true | all-gather | bytes 414720 | tf_op jit(solution)/shard_map/all_gather | solution.py:58
  113.3 6.8 %all-gather = bf16[4,288,144]{1,2,0:T(8,128)(2,1)S(1)} all-gather(bf16[1,288,144]{1,2,0:T(8,128)(2,1)S(1)} %copy.12), channel_id=1, replica_groups=mesh['shard'=8,'tensor'=4] {'tensor'}, dimensions={0}, use_global_device_ids=true | all-gather | bytes 414720 | tf_op jit(solution)/shard_map/all_gather | solution.py:57
  122.3 44.7 %all-gather.7.cloned.1.call-done = bf16[1152,1152]{1,0:T(8,128)(2,1)} async-done(((bf16[144,1152]{1,0:T(8,128)(2,1)}), bf16[1152,1152]{1,0:T(8,128)(2,1)}) %all-gather.7.cloned.1.call-update) | async-done | bytes 2654224 | tf_op jit(solution)/shard_map/all_gather | solution.py:62
  167.0 3.9 multiply_reduce_fusion
  171.6 2.4 fusion.2
  174.1 2.9 fusion.1
  177.0 3.9 fusion.8
  180.9 1.5 convolution_bitcast_fusion
  182.3 40.7 %all-gather.5.cloned.1.call-done = bf16[1152,1152]{1,0:T(8,128)(2,1)} async-done(((bf16[144,1152]{1,0:T(8,128)(2,1)}), bf16[1152,1152]{1,0:T(8,128)(2,1)}) %all-gather.5.cloned.1.call-update) | async-done | bytes 2654224 | tf_op jit(solution)/shard_map/all_gather | solution.py:61
  223.1 3.9 multiply_reduce_fusion.1
  227.7 2.2 fusion.4
  229.9 1.6 fusion.5
  231.5 1.6 fusion.6
  233.1 75.8 %all-reduce.2.cloned.1.call-done = f32[1152,288]{0,1:T(8,128)} async-done(((f32[1152,288]{0,1:T(8,128)}), f32[1152,288]{0,1:T(8,128)}) %all-reduce.2.cloned.1.call-update) | async-done | bytes 1327120 | tf_op jit(solution)/shard_map/psum | solution.py:74
  308.9 3.7 multiply_reduce_fusion.4
  312.5 40.0 %psum.23 = f32[]{:T(128)} all-reduce(f32[]{:T(128)} %get-tuple-element.22), channel_id=1, replica_groups=mesh['shard'=8,'tensor'=4] {'shard','tensor'}, use_global_device_ids=true, to_apply=%region_8.0 | all-reduce | flops 1 | bytes 8 | tf_op jit(solution)/shard_map/psum | solution.py:82
  354.0 32.4 %all_gather.27 = bf16[1152,288]{1,0:T(8,128)(2,1)S(1)} all-gather(bf16[144,288]{1,0:T(8,128)(2,1)S(1)} %get-tuple-element.8), channel_id=1, replica_groups=mesh['shard'=8,'tensor'=4] {'shard'}, dimensions={0}, use_global_device_ids=true | all-gather | bytes 746496 | tf_op jit(solution)/shard_map/all_gather | solution.py:86
  (47 shorter events, 12.0 us)
Async XLA Ops:
  7.2 10.5 %copy-start.4 = (bf16[256,288]{0,1:T(8,128)(2,1)S(1)}, bf16[256,288]{0,1:T(8,128)(2,1)}, u32[]{:S(2)}) copy-start(bf16[256,288]{0,1:T(8,128)(2,1)} %param.7) | copy-start | bytes 442372
  7.2 96.3 %reduce-scatter.4.cloned.1.call-start = ((), (), s32[]{:S(2)}) async-start(), calls=%async_computation.4 | async-start | bytes 3317760
  25.4 0.8 copy-start.2
  29.1 0.9 copy-start.3
  29.1 45.8 %copy-start.8 = (f32[2]{0:T(128)S(1)}, f32[2]{0:T(128)}, u32[]{:S(2)}) copy-start(f32[2]{0:T(128)} %param.10) | copy-start | bytes 28
  29.1 137.9 %all-gather.7.cloned.1.call-start = ((), (), s32[]{:S(2)}) async-start(), calls=%async_computation.2 | async-start | bytes 2985984 | tf_op jit(solution)/shard_map/all_gather | solution.py:62
  113.1 110.0 %all-gather.5.cloned.1.call-start = ((), (), s32[]{:S(2)}) async-start(), calls=%async_computation.1 | async-start | bytes 2985984 | tf_op jit(solution)/shard_map/all_gather | solution.py:61
  113.3 8.3 %copy-start.7 = (f32[4]{0:T(128)S(1)}, f32[4]{0:T(128)}, u32[]{:S(2)}) copy-start(f32[4]{0:T(128)} %param.11) | copy-start | bytes 52
  121.4 187.4 %all-reduce.2.cloned.1.call-start = ((), (), s32[]{:S(2)}) async-start(), calls=%async_computation.3 | async-start | bytes 2654208 | tf_op jit(solution)/shard_map/psum | solution.py:74
  167.0 4.6 %copy-start.1 = (bf16[1152,1152]{1,0:T(8,128)(2,1)S(1)}, bf16[1152,1152]{1,0:T(8,128)(2,1)}, u32[]{:S(2)}) copy-start(bf16[1152,1152]{1,0:T(8,128)(2,1)} %all-gather.7.cloned.1.call-done) | copy-start | bytes 7962628
  223.1 4.6 %copy-start = (bf16[1152,1152]{1,0:T(8,128)(2,1)S(1)}, bf16[1152,1152]{1,0:T(8,128)(2,1)}, u32[]{:S(2)}) copy-start(bf16[1152,1152]{1,0:T(8,128)(2,1)} %all-gather.5.cloned.1.call-done) | copy-start | bytes 7962628
  233.1 120.2 %copy-start.5 = (f32[144,288]{1,0:T(8,128)S(1)}, f32[144,288]{1,0:T(8,128)}, u32[]{:S(2)}) copy-start(f32[144,288]{1,0:T(8,128)} %param.9) | copy-start | bytes 497668
  233.1 120.2 %copy-start.6 = (bf16[144,288]{1,0:T(8,128)(2,1)S(1)}, bf16[144,288]{1,0:T(8,128)(2,1)}, u32[]{:S(2)}) copy-start(bf16[144,288]{1,0:T(8,128)(2,1)} %param.8) | copy-start | bytes 248836
Sparse Core Ops, SparseCore 0:
  29.2 74.2 reduce-scatter.3
  113.2 53.7 all-gather.6
  169.4 53.5 all-gather.4
  226.9 81.9 all-reduce.1
where the time goes:
time: 395 us; the launch traced here: 394 us
  waiting for transfers between devices  187 us (47%)
  blocking collectives  144 us (36%)
  matrix products  21.4 us (5%)
  between operations  18.6 us (5%)
  other arithmetic  11.5 us (3%)
  local copies, waits for them, and re-layouts  11.1 us (3%)
    psum x1, waiting for transfers between devices, on_device(): right_product = lax.psum(right_term, 'shard')  75.8 us
    all_gather x1, waiting for transfers between devices, on_device(): lax.all_gather(grad_wide, 'shard', axis=0, tiled=True)  44.7 us
    psum x1, blocking collectives, on_device(): traces = lax.psum(local_squares, ('shard', 'tensor'))  41.5 us
    all_gather x1, waiting for transfers between devices, on_device(): lax.all_gather(act_wide, 'shard', axis=0, tiled=True)  40.7 us
    psum x1, blocking collectives, on_device(): square_sum = lax.psum(jnp.sum(update * update), ('shard', 'tensor'))  40 us
    all_gather x1, blocking collectives, on_device(): gathered_weight = lax.all_gather(new_weight, 'shard', axis=0, tiled=True)  32.4 us
    unnamed x5, waiting for transfers between devices  25.6 us
    dot_general x5, matrix products, horner_columns(): jnp.dot(factor, iterate.astype(jnp.bfloat16), preferred_element_type=jnp....  10.7 us
  transfers between devices with their start and end apart: 4, of which 4 were waited for; matrix products, arithmetic and copies ran while one was open for 8% of the time, Pallas kernels for 0%

commit v1 on v0

--- a/solution.py
+++ b/solution.py
@@ -59,7 +59,12 @@
     )
     act_full, grad_full = (
         lax.all_gather(act_wide, "shard", axis=0, tiled=True),
-        lax.all_gather(grad_wide, "shard", axis=0, tiled=True),
+        jnp.concatenate(
+            jax.lax.all_to_all(
+                jnp.stack([grad_wide] * jax.lax.axis_size("shard"), axis=0), "shard", 0, 0
+            ),
+            axis=0,
+        ),
     )
     act_scale = jnp.sqrt(jnp.sum(jnp.square(act_full.astype(jnp.float32))))
     grad_scale = jnp.sqrt(jnp.sum(jnp.square(grad_full.astype(jnp.float32))))

time: 395 us -> 386 us (0.977)
  waiting for transfers between devices: 187 us -> 172 us
    all_to_all x0 -> x1, waiting for transfers between devices: none -> 75 us  [on_device(): jax.lax.all_to_all(jnp.stack([grad_wide] * jax.lax.axis_size('shard'), ax...]
    all_gather x1 -> x0, waiting for transfers between devices: 44.7 us -> none  [on_device(): lax.all_gather(grad_wide, 'shard', axis=0, tiled=True)]
    all_gather x1, waiting for transfers between devices: 40.7 us -> 0.02 us  [on_device(): lax.all_gather(act_wide, 'shard', axis=0, tiled=True)]
    psum x1, waiting for transfers between devices: 75.8 us -> 71.1 us  [on_device(): right_product = lax.psum(right_term, 'shard')]
    unnamed x5 -> x4, waiting for transfers between devices: 25.6 us -> 26.1 us
    unnamed x26 -> x24, local copies, waits for them, and re-layouts: 7.78 us -> 8.15 us
  transfers between devices with their start and end apart: 4 -> 4, of which waited for: 4 -> 3; matrix products, arithmetic and copies ran while one was open for 8% -> 8% of each run, Pallas kernels for 0% -> 0%
where the time goes in v1:
time: 386 us; the launch traced here: 385 us
  waiting for transfers between devices  172 us (45%)
  blocking collectives  144 us (37%)
  matrix products  22.4 us (6%)
  between operations  18.5 us (5%)
  local copies, waits for them, and re-layouts  14 us (4%)
  other arithmetic  9.51 us (2%)
  starting transfers between devices  4.03 us (1%)
    all_to_all x1, waiting for transfers between devices, on_device(): jax.lax.all_to_all(jnp.stack([grad_wide] * jax.lax.axis_size('shard'), ax...  75 us
    psum x1, waiting for transfers between devices, on_device(): right_product = lax.psum(right_term, 'shard')  71.1 us
    psum x1, blocking collectives, on_device(): traces = lax.psum(local_squares, ('shard', 'tensor'))  41.6 us
    psum x1, blocking collectives, on_device(): square_sum = lax.psum(jnp.sum(update * update), ('shard', 'tensor'))  40.1 us
    all_gather x1, blocking collectives, on_device(): gathered_weight = lax.all_gather(new_weight, 'shard', axis=0, tiled=True)  32.4 us
    unnamed x4, waiting for transfers between devices  26.1 us
    dot_general x5, matrix products, horner_columns(): jnp.dot(factor, iterate.astype(jnp.bfloat16), preferred_element_type=jnp....  11.5 us
    all_gather x1, blocking collectives, on_device(): lax.all_gather(acts, 'tensor', axis=1, tiled=True)  9.19 us
  transfers between devices with their start and end apart: 4, of which 3 were waited for; matrix products, arithmetic and copies ran while one was open for 8% of the time, Pallas kernels for 0%

profile of v1, /device:TPU:0, one launch (start us, length us, event | category | flops | bytes accessed | tf_op | source)
XLA Modules:
  0.0 385.0 jit_solution(11950317847489809245)
XLA Ops:
  7.2 9.2 %all_gather.18 = bf16[256,1152]{0,1:T(8,128)(2,1)S(1)} all-gather(bf16[256,288]{0,1:T(8,128)(2,1)} %param.6), channel_id=1, replica_groups=mesh['shard'=8,'tensor'=4] {'tensor'}, dimensions={1}, use_global_device_ids=true | all-gather | bytes 737280 | tf_op jit(solution)/shard_map/all_gather | solution.py:34
  17.7 7.6 %all_gather.19 = bf16[256,1152]{0,1:T(8,128)(2,1)S(1)} all-gather(bf16[256,288]{0,1:T(8,128)(2,1)S(1)} %copy-done.3), channel_id=1, replica_groups=mesh['shard'=8,'tensor'=4] {'tensor'}, dimensions={1}, use_global_device_ids=true | all-gather | bytes 737280 | tf_op jit(solution)/shard_map/all_gather | solution.py:35
  26.7 2.3 copy.24
  32.6 41.6 %psum.21 = f32[2]{0:T(128)S(1)} all-reduce(f32[2]{0:T(128)S(1)} %pad_maximum_fusion.1), channel_id=1, replica_groups=mesh['shard'=8,'tensor'=4] {'shard','tensor'}, use_global_device_ids=true, to_apply=%region_3.0 | all-reduce | flops 2 | bytes 16 | tf_op jit(solution)/shard_map/psum | solution.py:43
  78.0 26.1 %reduce-scatter.4.cloned.1.call-done = f32[144,576]{1,0:T(8,128)} async-done(((f32[1152,576]{1,0:T(8,128)}), f32[144,576]{1,0:T(8,128)}) %reduce-scatter.4.cloned.1.call-update) | async-done | bytes 331792
  105.8 6.7 %all-gather.1 = bf16[4,288,144]{1,2,0:T(8,128)(2,1)S(1)} all-gather(bf16[1,288,144]{1,2,0:T(8,128)(2,1)S(1)} %copy.21), channel_id=1, replica_groups=mesh['shard'=8,'tensor'=4] {'tensor'}, dimensions={0}, use_global_device_ids=true | all-gather | bytes 414720 | tf_op jit(solution)/shard_map/all_gather | solution.py:58
  113.0 1.7 stack.11
  114.7 3.7 all-to-all-start
  118.6 6.8 %all-gather = bf16[4,288,144]{1,2,0:T(8,128)(2,1)S(1)} all-gather(bf16[1,288,144]{1,2,0:T(8,128)(2,1)S(1)} %copy.19), channel_id=1, replica_groups=mesh['shard'=8,'tensor'=4] {'tensor'}, dimensions={0}, use_global_device_ids=true | all-gather | bytes 414720 | tf_op jit(solution)/shard_map/all_gather | solution.py:57
  126.3 2.1 reshape.17
  129.3 75.0 %all-to-all-done = bf16[8,144,1152]{2,1,0:T(8,128)(2,1)S(1)} async-done(((bf16[8,144,1152]{2,1,0:T(8,128)(2,1)}), bf16[8,144,1152]{2,1,0:T(8,128)(2,1)S(1)}, u32[]{:S(2)}, u32[]{:S(2)}) %all-to-all-start) | async-done | bytes 2654240 | tf_op jit(solution)/shard_map/all_to_all | solution.py:63
  204.3 2.0 multiply_reduce_fusion
  206.9 2.4 fusion.2
  209.3 3.0 fusion.1
  212.3 3.8 fusion.8
  216.1 1.5 convolution_bitcast_fusion
  217.7 3.9 %multiply_reduce_fusion.1 = f32[]{:T(128)} fusion(bf16[1152,1152]{1,0:T(8,128)(2,1)} %all-gather.4.cloned.1.call-done), kind=kLoop, calls=%fused_computation.1 | loop fusion | flops 3981311 | bytes 2654212 | tf_op jit(solution)/shard_map/reduce_sum | solution.py:69
  222.2 2.2 fusion.4
  224.4 1.7 fusion.5
  226.1 2.4 fusion.6
  228.4 71.1 %all-reduce.2.cloned.1.call-done = f32[1152,288]{0,1:T(8,128)} async-done(((f32[1152,288]{0,1:T(8,128)}), f32[1152,288]{0,1:T(8,128)}) %all-reduce.2.cloned.1.call-update) | async-done | bytes 1327120 | tf_op jit(solution)/shard_map/psum | solution.py:79
  299.5 3.9 %multiply_reduce_fusion.4 = (f32[]{:T(128)}, f32[144,288]{1,0:T(8,128)S(1)}) fusion(f32[1152,144]{0,1:T(8,128)} %fusion.6, f32[1152,288]{0,1:T(8,128)} %all-reduce.2.cloned.1.call-done), kind=kOutput, calls=%fused_computation.49 | convolution fusion | flops 573391872 | bytes 2156548 | tf_op jit(solution)/shard_map/dot_general | solution.py:80
  303.4 40.1 %psum.23 = f32[]{:T(128)} all-reduce(f32[]{:T(128)} %get-tuple-element.24), channel_id=1, replica_groups=mesh['shard'=8,'tensor'=4] {'shard','tensor'}, use_global_device_ids=true, to_apply=%region_8.0 | all-reduce | flops 1 | bytes 8 | tf_op jit(solution)/shard_map/psum | solution.py:87
  344.9 32.4 %all_gather.23 = bf16[1152,288]{1,0:T(8,128)(2,1)S(1)} all-gather(bf16[144,288]{1,0:T(8,128)(2,1)S(1)} %get-tuple-element.10), channel_id=1, replica_groups=mesh['shard'=8,'tensor'=4] {'shard'}, dimensions={0}, use_global_device_ids=true | all-gather | bytes 746496 | tf_op jit(solution)/shard_map/all_gather | solution.py:91
  (45 shorter events, 13.6 us)
Async XLA Ops:
  7.2 10.5 %copy-start.3 = (bf16[256,288]{0,1:T(8,128)(2,1)S(1)}, bf16[256,288]{0,1:T(8,128)(2,1)}, u32[]{:S(2)}) copy-start(bf16[256,288]{0,1:T(8,128)(2,1)} %param.7) | copy-start | bytes 442372
  7.2 96.9 %reduce-scatter.4.cloned.1.call-start = ((), (), s32[]{:S(2)}) async-start(), calls=%async_computation.4 | async-start | bytes 3317760
  25.4 0.8 copy-start.1
  29.1 0.9 copy-start.2
  29.1 45.8 %copy-start.7 = (f32[2]{0:T(128)S(1)}, f32[2]{0:T(128)}, u32[]{:S(2)}) copy-start(f32[2]{0:T(128)} %param.10) | copy-start | bytes 28
  114.7 89.6 %all-to-all-start = ((bf16[8,144,1152]{2,1,0:T(8,128)(2,1)}), bf16[8,144,1152]{2,1,0:T(8,128)(2,1)S(1)}, u32[]{:S(2)}, u32[]{:S(2)}) async-start(bf16[8,144,1152]{2,1,0:T(8,128)(2,1)} %stack.11), calls=%async_computation | async-start | bytes 5308416 | tf_op jit(solution)/shard_map/all_to_all | solution.py:63
  118.4 99.2 %all-gather.4.cloned.1.call-start = ((), (), s32[]{:S(2)}) async-start(), calls=%async_computation.2 | async-start | bytes 2985984 | tf_op jit(solution)/shard_map/all_gather | solution.py:61
  118.6 10.1 %copy-start.6 = (f32[4]{0:T(128)S(1)}, f32[4]{0:T(128)}, u32[]{:S(2)}) copy-start(f32[4]{0:T(128)} %param.11) | copy-start | bytes 52
  128.4 171.1 %all-reduce.2.cloned.1.call-start = ((), (), s32[]{:S(2)}) async-start(), calls=%async_computation.3 | async-start | bytes 2654208 | tf_op jit(solution)/shard_map/psum | solution.py:79
  217.6 4.6 %copy-start = (bf16[1152,1152]{1,0:T(8,128)(2,1)S(1)}, bf16[1152,1152]{1,0:T(8,128)(2,1)}, u32[]{:S(2)}) copy-start(bf16[1152,1152]{1,0:T(8,128)(2,1)} %all-gather.4.cloned.1.call-done) | copy-start | bytes 7962628
  228.4 115.7 %copy-start.4 = (f32[144,288]{1,0:T(8,128)S(1)}, f32[144,288]{1,0:T(8,128)}, u32[]{:S(2)}) copy-start(f32[144,288]{1,0:T(8,128)} %param.9) | copy-start | bytes 497668
  228.4 115.7 %copy-start.5 = (bf16[144,288]{1,0:T(8,128)(2,1)S(1)}, bf16[144,288]{1,0:T(8,128)(2,1)}, u32[]{:S(2)}) copy-start(bf16[144,288]{1,0:T(8,128)(2,1)} %param.8) | copy-start | bytes 248836
Sparse Core Ops, SparseCore 0:
  29.2 74.8 reduce-scatter.3
  128.5 83.1 all-gather.3
  217.7 81.7 all-reduce.1
